TPU v7x, 128 devices: a whole 4x4x4 slice. The times are simulated.
128 devices in a mesh: row: 16 (over z_hi, x, core), col: 8 (over y, z_lo).
Axes of the slice: x: 4, y: 4, z: 4 (z_hi: 2, z_lo: 2; z = z_hi * 2 + z_lo), core: 2. Of those that a mesh axis runs over, the one named last changes fastest.
Arguments:
- a_blocks: bfloat16 [128, 128, 9216], P('row', 'col'), may hold values from -0.625 to 0.625
- a_mask: int32 [128, 128], P('row', 'col'), may hold values from 0 to 1, as said below
- p_blocks: bfloat16 [128, 64, 9216], P('row', 'col'), may hold values from -3 to 3
- p_mask: int32 [128, 64], P('row', 'col'), may hold values from 0 to 1, as said below
- section_owner: int32 [2], replicated, may hold values from 0 to 7, as said below
- agg_order: int32 [64], replicated, may hold values from 0 to 63, as said below
Outputs:
- coarse: float32 [6144, 6144], P(('row', 'col'))
Inputs may be any that keep to these rules, and one draw needn't show every extreme that they name: `a_mask`: each tile of 8 x 16 blocks (the fine block rows of one index of row and the fine block columns of one index of col) holds between 32 and 96 ones, and in every index of row some tile holds exactly 96. `section_owner`: distinct indices of col; one of the sections takes index 7. `agg_order`: each coarse block once. `p_mask`: with c = i // 2: fine block row i feeds aggregate agg_order[c] always, agg_order[c - 1] and agg_order[c + 1] possibly, agg_order[(c + 32) mod 64] always where i is a multiple of 2, aggregate ((i // 16 + 8 // 2) mod 8) * 8 + (i mod 8) always, and nothing else.
All inputs are finite; a program needn't handle non-finite values.
Results may differ from a plain program's by a relative error of at most 0.0029.
Values may be sent and summed in bfloat16 or wider, within the bound.
No kernel may reach another device: no remote copies, remote signals or barrier semaphores. Data moves between devices by JAX's collectives and lax.ppermute only.
A program may use at most 128 MiB of HBM per device.

v0:
```python
import jax
import jax.numpy as jnp
from jax import lax
from jax.sharding import PartitionSpec as P

BS = 96
SECTIONS = 2


def spread(value, axis, source):
    kept = jnp.where(lax.axis_index(axis) == source, value, 0).astype(value.dtype)
    return lax.psum(kept, axis)


def body(a_blocks, a_mask, p_blocks, p_mask, section_owner, agg_order):
    block_rows, block_cols, block_area = a_blocks.shape
    coarse_cols = p_blocks.shape[1]
    fine_operator = a_blocks * a_mask[:, :, None].astype(jnp.bfloat16)
    prolongation = p_blocks * p_mask[:, :, None].astype(jnp.bfloat16)
    groups = lax.axis_size("row") // lax.axis_size("col")
    product = jnp.zeros((block_rows, BS, coarse_cols, BS), jnp.float32)
    for section_num in range(SECTIONS):
        section_root = section_owner[section_num]
        operator_panel = spread(fine_operator, "col", section_root)
        pieces = []
        for member in range(groups):
            pieces.append(spread(prolongation, "row", section_root * groups + member))
        prolong_panel = jnp.concatenate(pieces, axis=0)
        product = product + jnp.einsum(
            "ikab,kjbc->iajc",
            operator_panel.reshape(block_rows, block_cols, BS, BS),
            prolong_panel.reshape(block_cols, coarse_cols, BS, BS),
            preferred_element_type=jnp.float32,
        )
    fine_coarse = product.reshape(block_rows, BS, coarse_cols * BS).astype(jnp.bfloat16)
    prolong_rows = lax.all_gather(prolongation, "col", axis=1, tiled=True)
    total_blocks = prolong_rows.shape[1]
    prolong_four = prolong_rows.reshape(block_rows, total_blocks, BS, BS)
    share = total_blocks * BS // lax.axis_size("row")
    selected = jnp.take(prolong_four, agg_order, axis=1)
    partial_sum = jnp.einsum(
        "iIab,iaj->Ibj", selected, fine_coarse, preferred_element_type=jnp.float32
    )
    summed = lax.psum_scatter(
        partial_sum.reshape(share * lax.axis_size("row"), coarse_cols * BS),
        "row",
        scatter_dimension=0,
        tiled=True,
    )
    return lax.all_to_all(summed, "col", split_axis=0, concat_axis=1, tiled=True)


def solution(mesh):
    in_specs = (
        P("row", "col", None),
        P("row", "col"),
        P("row", "col", None),
        P("row", "col"),
        P(),
        P(),
    )
    out_specs = P(("row", "col"), None)
    return jax.shard_map(body, mesh=mesh, in_specs=in_specs, out_specs=out_specs, check_vma=False)
```

profile of v0, /device:TPU:0, one launch (start us, length us, event | category | flops | bytes accessed | tf_op | source)
XLA Modules:
  0.0 909.4 jit_solution(15240294089234906260)
XLA Ops:
  6.5 0.0 all-reduce.5.cloned.1.call-start
  6.5 1.3 fusion.7
  9.1 0.7 convert_element_type.22
  9.7 2.5 broadcast_select_fusion.5
  12.3 0.0 copy-start
  12.3 2.0 broadcast_select_fusion.4
  14.2 0.3 copy-done
  14.5 0.0 copy-start.2
  14.5 0.0 all-reduce.5.cloned.1.call-update
  14.5 0.0 all-reduce.7.cloned.1.call-start
  15.7 0.0 copy-done.2
  15.8 3.5 broadcast_select_fusion.1
  19.2 5.7 reshape.32
  24.9 4.1 reshape.34
  29.0 0.0 copy-start.4
  29.0 0.0 all-reduce.7.cloned.1.call-update
  29.0 0.0 all-gather.2.cloned.1.call-start
  29.1 0.7 all-gather.2.cloned.1.call-update
  29.8 0.2 reduce-scatter.2.cloned.1.call-start
  30.0 0.0 copy-done.4
  30.1 139.7 %all-reduce.5.cloned.1.call-done = (bf16[8,8,9216]{2,1,0:T(8,128)(2,1)}, bf16[8,8,9216]{2,1,0:T(8,128)(2,1)}, bf16[8,8,9216]{2,1,0:T(8,128)(2,1)}, bf16[8,8,9216]{2,1,0:T(8,128)(2,1)}) async-done(((bf16[8,8,9216]{2,1,0:T(8,128)(2,1)}, bf16[8,8,9216]{2,1,0:T(8,128)(2,1)}, bf16[8,8,9216]{2,1,0:T(8,128)(2,1)}, bf16[8,8,9216]{2,1,0:T(8,128)(2,1)}), (bf16[8,8,9216]{2,1,0:T(8,128)(2,1)}, ...) | async-done | bytes 4718608 | tf_op jit(solution)/shard_map/psum | solution.py:12
  169.8 2.5 pad_maximum_fusion
  172.3 2.8 copy.12
  175.1 5.7 reshape.46
  180.8 2.8 copy.13
  183.6 4.5 reshape.49
  188.0 245.6 %all-reduce.7.cloned.1.call-done = (bf16[8,16,96,96]{3,2,1,0:T(8,128)(2,1)}, bf16[8,16,96,96]{3,2,1,0:T(8,128)(2,1)}) async-done(((bf16[8,16,96,96]{3,2,1,0:T(8,128)(2,1)}, bf16[8,16,96,96]{3,2,1,0:T(8,128)(2,1)}), (bf16[8,16,96,96]{3,2,1,0:T(8,128)(2,1)}, bf16[8,16,96,96]{3,2,1,0:T(8,128)(2,1)})) %all-reduce.7.cloned.1.call-update) | async-done | bytes 4718608 | tf_op jit(solution)/shard_map/psum | solution.py:12
  433.6 0.0 copy-start.1
  433.6 0.0 copy-start.3
  433.6 4.5 fusion
  438.1 0.0 copy-done.1
  438.2 0.0 copy-done.3
  438.2 2.7 fusion.4
  440.8 0.6 copy.14
  441.5 1.3 convert_element_type.25
  442.8 182.6 %all-gather.2.cloned.1.call-done = bf16[8,64,9216]{2,1,0:T(8,128)(2,1)} async-done(((bf16[8,8,9216]{2,1,0:T(8,128)(2,1)}), bf16[8,64,9216]{2,1,0:T(8,128)(2,1)}) %all-gather.2.cloned.1.call-update) | async-done | bytes 9437200 | tf_op jit(solution)/shard_map/all_gather | solution.py:36
  625.4 18.7 %reshape.31 = bf16[8,64,96,96]{3,2,1,0:T(8,128)(2,1)} reshape(bf16[8,64,9216]{2,1,0:T(8,128)(2,1)} %all-gather.2.cloned.1.call-done) | data formatting | bytes 18874368 | tf_op jit(solution)/shard_map/reshape | solution.py:38
  644.1 11.8 %gather_fusion = bf16[64,8,96,96]{3,2,1,0:T(8,128)(2,1)} fusion(bf16[8,64,96,96]{3,2,1,0:T(8,128)(2,1)} %reshape.31, s32[1024]{0:T(1024)S(1)} %pad_clamp_fusion), kind=kCustom, calls=%fused_computation | custom fusion | bytes 18874624 | tf_op jit(solution)/shard_map/jit(_take)/gather | solution.py:40
  655.9 6.7 select_bitcast_fusion
  662.6 23.4 %copy.11 = bf16[64,96,96,8]{1,0,2,3:T(8,128)(2,1)} copy(bf16[64,96,96,8]{1,2,3,0:T(8,128)(2,1)S(1)} %select_bitcast_fusion) | data formatting | bytes 18874368 | tf_op jit(solution)/shard_map/jit(_take)/select_n | solution.py:40
  686.0 22.8 %dot_general.11 = bf16[6144,96,8]{0,1,2:T(8,128)(2,1)} reshape(bf16[64,96,96,8]{1,0,2,3:T(8,128)(2,1)} %copy.11) | data formatting | bytes 18874368 | tf_op jit(solution)/shard_map/iIab,iaj->Ibj/dot_general | solution.py:41
  708.8 14.5 %convolution_bitcast_fusion = f32[6144,768]{1,0:T(8,128)} fusion(bf16[6144,96,8]{0,1,2:T(8,128)(2,1)} %dot_general.11, bf16[8,96,768]{2,1,0:T(8,128)(2,1)S(1)} %convert_element_type.25), kind=kOutput, calls=%fused_computation.2 | convolution fusion | flops 7247757312 | bytes 29491200 | tf_op jit(solution)/shard_map/iIab,iaj->Ibj/dot_general | solution.py:41
  723.3 0.0 reduce-scatter.2.cloned.1.call-update
  723.3 157.8 %reduce-scatter.2.cloned.1.call-done = f32[384,768]{1,0:T(8,128)} async-done(((f32[6144,768]{1,0:T(8,128)}), f32[384,768]{1,0:T(8,128)}) %reduce-scatter.2.cloned.1.call-update) | async-done | bytes 1179664 | tf_op jit(solution)/shard_map/reduce_scatter | solution.py:44
  881.1 20.6 %all_to_all.19 = f32[8,48,768]{2,1,0:T(8,128)S(1)} all-to-all(f32[8,48,768]{2,1,0:T(8,128)} %bitcast.45), channel_id=1, replica_groups=mesh['row'=16,'col'=8] {'col'}, dimensions={0} | all-to-all | bytes 2359296 | tf_op jit(solution)/shard_map/all_to_all | solution.py:50
  901.7 1.1 copy.20
  (4 shorter events, 0.0 us)
Async XLA Ops:
  6.5 163.2 %all-reduce.5.cloned.1.call-start = ((), (), s32[]{:S(2)}) async-start(), calls=%async_computation.4 | async-start | bytes 9437184 | tf_op jit(solution)/shard_map/psum | solution.py:12
  12.3 2.2 copy-start
  14.5 1.3 copy-start.2
  14.5 419.1 %all-reduce.7.cloned.1.call-start = ((), (), s32[]{:S(2)}) async-start(), calls=%async_computation.5 | async-start | bytes 12582912 | tf_op jit(solution)/shard_map/psum | solution.py:12
  29.0 1.0 copy-start.4
  29.0 596.4 %all-gather.2.cloned.1.call-start = ((), (), s32[]{:S(2)}) async-start(), calls=%async_computation.2 | async-start | bytes 10616832 | tf_op jit(solution)/shard_map/all_gather | solution.py:36
  29.8 851.4 %reduce-scatter.2.cloned.1.call-start = ((), (), s32[]{:S(2)}) async-start(), calls=%async_computation.3 | async-start | bytes 20054016 | tf_op jit(solution)/shard_map/reduce_scatter | solution.py:44
  433.6 4.5 copy-start.1
  433.6 4.5 copy-start.3
Sparse Core Ops, SparseCore 0:
  14.6 155.1 all-reduce.4
  172.3 261.2 all-reduce.6
  435.3 190.0 all-gather.1
  723.4 157.6 reduce-scatter.1
where the time goes:
time: 911 us; the launch traced here: 909 us
  waiting for transfers between devices  726 us (80%)
  local copies, waits for them, and re-layouts  107 us (12%)
  matrix products  21.7 us (2%)
  blocking collectives  20.6 us (2%)
  other arithmetic  17.9 us (2%)
  between operations  15.7 us (2%)
    psum x2, waiting for transfers between devices, spread(): return lax.psum(kept, axis)  385 us
    all_gather x1, waiting for transfers between devices, body(): prolong_rows = lax.all_gather(prolongation, 'col', axis=1, tiled=True)  183 us
    reduce_scatter x1, waiting for transfers between devices, body(): lax.psum_scatter(partial_sum.reshape(share * lax.axis_size('row'), coarse...  158 us
    select_n x1, local copies, waits for them, and re-layouts, body(): selected = jnp.take(prolong_four, agg_order, axis=1)  23.4 us
    dot_general x1, local copies, waits for them, and re-layouts, body(): jnp.einsum('iIab,iaj->Ibj', selected, fine_coarse, preferred_element_type...  22.8 us
    all_to_all x1, blocking collectives, body(): lax.all_to_all(summed, 'col', split_axis=0, concat_axis=1, tiled=True)  20.6 us
    reshape x1, local copies, waits for them, and re-layouts, body(): prolong_four = prolong_rows.reshape(block_rows, total_blocks, BS, BS)  18.7 us
  transfers between devices with their start and end apart: 4, of which 4 were waited for; matrix products, arithmetic and copies ran while one was open for 4% of the time, Pallas kernels for 0%

commit v1 on v0

v1 whole, which is shorter than its diff:
```python
import jax
import jax.numpy as jnp
from jax import lax
from jax.experimental import pallas as pl
from jax.experimental.pallas import tpu as pltpu
from jax.sharding import PartitionSpec as P

BS = 96
BR = 8
NCB = 64
KK = 4
WIDE = KK * BS
ROWS = 16
COLS = 8
PIECE = BS // ROWS
SLOTS = 16
LANES = PIECE * WIDE
USLOTS = 5
PW = 512
OUTSLOTS = 18
F32 = jnp.float32
BF16 = jnp.bfloat16


def lookup(table, index):
    hit = index[..., None] == jnp.arange(table.shape[0], dtype=jnp.int32)
    return jnp.sum(jnp.where(hit, table, 0), axis=-1)


def band_columns(rows, agg_order):
    center = rows // 2
    places = jnp.stack(
        [(center + NCB - 1) % NCB, center, (center + 1) % NCB, (center + NCB // 2) % NCB], axis=-1
    )
    return lookup(agg_order, places)


def partial_kernel(p_ref, mine_ref, a_ref, x_ref, own_ref, scr):
    seen = set()
    for i in range(BR):
        q = lax.dot_general(
            p_ref[i], a_ref[i], (((0,), (0,)), ((), ())), preferred_element_type=F32
        )
        local = i // 2
        for u in range(3):
            w = local + u
            value = q[u * BS : (u + 1) * BS]
            ref, at = (scr, 0) if w == 0 else (scr, 1) if w == 5 else (own_ref, w - 1)
            if w in seen:
                ref[at] += value
            else:
                ref[at] = value
                seen.add(w)
        if i % 2 == 0:
            scr[2 + local] = q[3 * BS : 4 * BS]
        scr[6 + i] = q[4 * BS : 5 * BS]
    mine = mine_ref[...].astype(F32)
    scr[14] = mine[:, :WIDE]
    scr[15, :, : PW - WIDE] = mine[:, WIDE:]
    scr[15, :, PW - WIDE :] = jnp.zeros((BS, 2 * WIDE - PW), F32)
    for octet in range(BS // 8):
        chunk = jnp.swapaxes(scr[:, octet * 8 : octet * 8 + 8, :], 0, 1)
        for e in range(8):
            j, pp = divmod(octet * 8 + e, PIECE)
            x_ref[j, :, pp * WIDE : (pp + 1) * WIDE] = chunk[e].astype(BF16)


def product_kernel(r_ref, own_ref, x_ref, scr, held):
    for octet in range(BS // 8):
        rows = []
        for e in range(8):
            j, pp = divmod(octet * 8 + e, PIECE)
            rows.append(r_ref[j, :, pp * WIDE : (pp + 1) * WIDE].astype(F32))
        scr[:, octet * 8 : octet * 8 + 8, :] = jnp.swapaxes(jnp.stack(rows), 0, 1)
    for kk in range(KK):
        right = jnp.concatenate([scr[8 + 2 * kk], scr[9 + 2 * kk][:, :BS]], axis=1).astype(BF16)
        for t in range(4):
            g = (own_ref[t] + scr[t] + scr[4 + t])[:, kk * BS : (kk + 1) * BS]
            high = g.astype(BF16)
            low = (g - high.astype(F32)).astype(BF16)
            out = jnp.dot(high, right, preferred_element_type=F32)
            out = out + jnp.dot(low, right, preferred_element_type=F32)
            span = slice(t * BS, (t + 1) * BS)
            x_ref[span, kk * WIDE : (kk + 1) * WIDE] = out[:, :WIDE].astype(BF16)
            if kk % 2 == 0:
                held[t] = out[:, WIDE:]
            else:
                sec = kk // 2
                cross = held[t] + out[:, WIDE:]
                x_ref[span, 4 * WIDE + sec * BS : 4 * WIDE + (sec + 1) * BS] = cross.astype(BF16)


def place_kernel(j_ref, r_ref, out_ref, acc):
    acc[...] = jnp.zeros_like(acc)

    def step(c, carry):
        for s in range(OUTSLOTS):
            at = j_ref[c, s]
            acc[at] += r_ref[c, :, s * BS : (s + 1) * BS].astype(F32)
        return carry

    lax.fori_loop(0, COLS, step, 0)
    for block in range(NCB):
        out_ref[:, block * BS : (block + 1) * BS] = acc[block]


VMEM = pl.BlockSpec(memory_space=pltpu.VMEM)
SMEM = pl.BlockSpec(memory_space=pltpu.SMEM)


def body(a_blocks, a_mask, p_blocks, p_mask, section_owner, agg_order):
    area = a_blocks.shape[2]
    row, col = lax.axis_index("row"), lax.axis_index("col")
    rows = row * BR + jnp.arange(BR, dtype=jnp.int32)

    band = band_columns(rows, agg_order)
    cross = ((rows // 16 + 4) % COLS) * BR + rows % BR
    live = jnp.stack([jnp.ones_like(rows)] * 3 + [1 - rows % 2], axis=-1) > 0
    fresh = ~jnp.any((band == cross[:, None]) & live, axis=1)
    wanted = jnp.concatenate([band, cross[:, None]], axis=1)
    usable = jnp.concatenate([live, fresh[:, None]], axis=1)
    local = wanted[:, :, None] == col * BR + jnp.arange(BR, dtype=jnp.int32)
    pick = local & usable[:, :, None] & (p_mask[:, None, :] != 0)
    compact = jnp.einsum(
        "iuj,ijf->iuf", pick.astype(BF16), p_blocks, preferred_element_type=F32
    ).astype(BF16)

    masked = a_blocks * a_mask[:, :, None].astype(BF16)
    tiles = masked.reshape(BR, 2, COLS, area).transpose(2, 0, 1, 3).reshape(COLS, 2 * BR, area)
    first = lax.all_to_all(jnp.concatenate([tiles, compact], axis=1), "col", 0, 0, tiled=True)

    mine = jnp.sum(first[:, 2 * BR :].astype(F32), axis=0).astype(BF16)
    mine = mine.reshape(USLOTS, BS, BS).transpose(1, 0, 2).reshape(BS, USLOTS * BS)
    mine = jnp.pad(mine, ((0, 0), (0, PW - USLOTS * BS)))
    p_rows = lax.all_to_all(
        jnp.broadcast_to(mine[None], (COLS, BS, PW)), "col", 0, 0, tiled=True
    )

    parts = [
        lax.dynamic_index_in_dim(first, section_owner[s], 0, keepdims=False)[: 2 * BR]
        for s in range(2)
    ]
    a_part = jnp.stack(parts).reshape(2, BR, 2, BS, BS).transpose(1, 3, 0, 2, 4).reshape(BR, BS, WIDE)

    spread, own = pl.pallas_call(
        partial_kernel,
        out_shape=(
            jax.ShapeDtypeStruct((ROWS, SLOTS, LANES), BF16),
            jax.ShapeDtypeStruct((4, BS, WIDE), F32),
        ),
        in_specs=[VMEM] * 3,
        out_specs=(VMEM, VMEM),
        scratch_shapes=[pltpu.VMEM((SLOTS, BS, WIDE), F32)],
        name="partial",
    )(p_rows, mine, a_part)
    spread = lax.all_to_all(spread, "row", 0, 0, tiled=True)

    every = jnp.arange(ROWS, dtype=jnp.int32)[:, None]
    slot = jnp.arange(SLOTS, dtype=jnp.int32)[None, :]
    target = jnp.where(
        slot == 0,
        (4 * every + NCB - 1) % NCB,
        jnp.where(slot == 1, (4 * every + 4) % NCB, (4 * every + slot - 2 + NCB // 2) % NCB),
    )
    source = jnp.where(slot < 6, lookup(agg_order, target), ((every // 2 + 4) % COLS) * BR + slot - 6)
    source = jnp.where(slot < 14, source, -1).reshape(-1)
    from_row = (jnp.broadcast_to(every, (ROWS, SLOTS)) * SLOTS + slot).reshape(-1)
    home = agg_order.reshape(ROWS, 4)
    near = jnp.concatenate([home, home, jnp.full((ROWS, 8), -2, jnp.int32)], axis=1).reshape(-1)
    tail = jnp.arange(8, dtype=jnp.int32)
    panel = (2 * lookup(section_owner, tail // 4) + (tail // 2) % 2) * SLOTS + 14 + tail % 2
    panel = jnp.concatenate([jnp.full((8,), -1, jnp.int32), panel])
    panel = jnp.broadcast_to(panel[None], (ROWS, SLOTS)).reshape(-1)
    choose = (near[:, None] == source[None]) | (panel[:, None] == from_row[None])
    total = jnp.dot(
        choose.astype(BF16), spread.reshape(ROWS * SLOTS, LANES), preferred_element_type=F32
    )
    high = total.astype(BF16)
    low = (total - high.astype(F32)).astype(BF16)
    is_low = (jnp.arange(ROWS * SLOTS) % SLOTS // 4 == 1)[:, None]
    back = jnp.where(is_low, low, high).reshape(ROWS, SLOTS, LANES)
    back = lax.all_to_all(back, "row", 0, 0, tiled=True)

    outs = pl.pallas_call(
        product_kernel,
        out_shape=jax.ShapeDtypeStruct((4 * BS, OUTSLOTS * BS), BF16),
        in_specs=[VMEM] * 2,
        out_specs=VMEM,
        scratch_shapes=[pltpu.VMEM((SLOTS, BS, WIDE), F32), pltpu.VMEM((4, BS, BS), F32)],
        name="product",
    )(back, own)
    outs = lax.all_to_all(outs.reshape(COLS, 4 * BS // COLS, OUTSLOTS * BS), "col", 0, 0, tiled=True)

    k_col = jnp.arange(COLS, dtype=jnp.int32)[:, None, None]
    k_sec = section_owner[None, :, None]
    k_half = jnp.arange(2, dtype=jnp.int32)[None, None, :]
    k_rows = 2 * BR * k_sec + BR * k_half + k_col
    j_band = band_columns(k_rows, agg_order).reshape(COLS, 4 * KK)
    j_cross = ((k_sec + 4) % COLS)[:, :, 0] * BR + k_col[:, :, 0]
    j_table = jnp.concatenate([j_band, j_cross], axis=1)
    return pl.pallas_call(
        place_kernel,
        out_shape=jax.ShapeDtypeStruct((4 * BS // COLS, NCB * BS), F32),
        in_specs=[SMEM, VMEM],
        out_specs=VMEM,
        scratch_shapes=[pltpu.VMEM((NCB, 4 * BS // COLS, BS), F32)],
        name="place",
    )(j_table, outs)


def solution(mesh):
    in_specs = (
        P("row", "col", None),
        P("row", "col"),
        P("row", "col", None),
        P("row", "col"),
        P(),
        P(),
    )
    out_specs = P(("row", "col"), None)
    return jax.shard_map(body, mesh=mesh, in_specs=in_specs, out_specs=out_specs, check_vma=False)
```

time: 911 us -> 173 us (0.19)
  waiting for transfers between devices: 726 us -> 92.3 us
  local copies, waits for them, and re-layouts: 107 us -> 10 us
  matrix products: 21.7 us -> 1.06 us
  starting transfers between devices: 0.3 us -> 20.6 us
  Pallas kernels: 0 us -> 11.7 us
  between operations: 15.7 us -> 4.03 us
    psum x2 -> x0, waiting for transfers between devices: 385 us -> none  [spread(): return lax.psum(kept, axis)]
    all_gather x1 -> x0, waiting for transfers between devices: 183 us -> none  [body(): prolong_rows = lax.all_gather(prolongation, 'col', axis=1, tiled=True)]
    reduce_scatter x1 -> x0, waiting for transfers between devices: 158 us -> none  [body(): lax.psum_scatter(partial_sum.reshape(share * lax.axis_size('row'), coarse...]
    all_to_all x0 -> x4, waiting for transfers between devices: none -> 92.3 us  [the longest x1 45.8 us: body(): lax.all_to_all(jnp.concatenate([tiles, compact], axis=1), 'col', 0, 0, ti...]
    reshape x5 -> x6, local copies, waits for them, and re-layouts: 38.6 us -> 3.06 us  [the longest x1 1.36 us: body(): jnp.stack(parts).reshape(2, BR, 2, BS, BS).transpose(1, 3, 0, 2, 4)]
    select_n x1, local copies, waits for them, and re-layouts: 23.4 us -> 0.08 us  [body(): source = jnp.where(slot < 14, source, -1).reshape(-1)]
    dot_general x1 -> x0, local copies, waits for them, and re-layouts: 22.8 us -> none  [body(): jnp.einsum('iIab,iaj->Ibj', selected, fine_coarse, preferred_element_type...]
    dot_general x3 -> x2, matrix products: 21.7 us -> 1.06 us  [the longest x1 0.53 us: body(): jnp.dot(choose.astype(BF16), spread.reshape(ROWS * SLOTS, LANES), preferr...]
where the time goes in v1:
time: 173 us
  waiting for transfers between devices  92.3 us (53%)
  blocking collectives  22.4 us (13%)
  starting transfers between devices  20.6 us (12%)
  Pallas kernels  11.7 us (7%)
  other arithmetic  10.5 us (6%)
  local copies, waits for them, and re-layouts  10 us (6%)
  between operations  4.03 us (2%)
    all_to_all x1, waiting for transfers between devices, body(): lax.all_to_all(jnp.concatenate([tiles, compact], axis=1), 'col', 0, 0, ti...  45.8 us
    all_to_all x1, blocking collectives, body(): back = lax.all_to_all(back, 'row', 0, 0, tiled=True)  22.4 us
    all_to_all x1, waiting for transfers between devices, body(): lax.all_to_all(outs.reshape(COLS, 4 * BS // COLS, OUTSLOTS * BS), 'col',...  20.4 us
    all_to_all x1, waiting for transfers between devices, body(): spread = lax.all_to_all(spread, 'row', 0, 0, tiled=True)  18.4 us
    all_to_all x1, waiting for transfers between devices, body(): lax.all_to_all(jnp.broadcast_to(mine[None], (COLS, BS, PW)), 'col', 0, 0,...  7.6 us
    all_to_all x1, starting transfers between devices, body(): spread = lax.all_to_all(spread, 'row', 0, 0, tiled=True)  7.43 us
    all_to_all x1, starting transfers between devices, body(): lax.all_to_all(jnp.concatenate([tiles, compact], axis=1), 'col', 0, 0, ti...  6.07 us
    pallas_call x1, Pallas kernels, body(): pl.pallas_call(place_kernel, out_shape=jax.ShapeDtypeStruct((4 * BS // CO...  4.11 us
  transfers between devices with their start and end apart: 4, of which 4 were waited for; matrix products, arithmetic and copies ran while one was open for 4% of the time, Pallas kernels for 0%

profile of v1, /device:TPU:0, one launch (start us, length us, event | category | flops | bytes accessed | tf_op | source)
XLA Modules:
  0.0 172.6 jit_solution(5021971916685460686)
XLA Ops:
  0.0 0.0 copy-start
  0.1 0.9 select_reduce_fusion.2
  1.1 0.1 pad.13.clone
  1.1 0.1 and_reduce_fusion
  1.3 0.1 copy.19
  1.4 0.1 copy.18
  1.5 0.7 broadcast_compare_fusion
  2.1 0.7 convert_element_type.22
  2.8 1.9 %broadcast_multiply_fusion = bf16[8,16,9216]{2,1,0:T(8,128)(2,1)S(1)} fusion(bf16[8,16,9216]{2,1,0:T(8,128)(2,1)} %param.6, bf16[8,16]{1,0:T(8,128)(2,1)S(1)} %convert_element_type.22), kind=kLoop, calls=%fused_computation.5 | loop fusion | flops 1179648 | bytes 4718848 | tf_op jit(solution)/shard_map/mul | solution.py:128
  4.7 1.3 copy.23
  6.0 0.0 copy-done
  6.0 0.5 convolution_convert_fusion
  6.6 2.2 %pad_maximum_fusion = bf16[8,21,9216]{2,1,0:T(8,128)(2,1)} fusion(bf16[8,5,9216]{2,1,0:T(8,128)(2,1)S(1)} %convolution_convert_fusion, bf16[8,16,9216]{2,1,0:T(8,128)(2,1)S(1)} %copy.23), kind=kLoop, calls=%fused_computation.1 | loop fusion | flops 6193152 | bytes 6193152 | tf_op jit(solution)/shard_map/concatenate | solution.py:130
  8.8 0.0 copy-start.5
  8.8 0.0 copy-start.4
  8.8 6.1 %all-to-all-start = ((bf16[8,21,9216]{2,1,0:T(8,128)(2,1)}), bf16[8,21,9216]{2,1,0:T(8,128)(2,1)}, u32[]{:S(2)}, u32[]{:S(2)}) async-start(bf16[8,21,9216]{2,1,0:T(8,128)(2,1)} %pad_maximum_fusion), calls=%async_computation | async-start | bytes 7077888 | tf_op jit(solution)/shard_map/all_to_all | solution.py:130
  14.9 0.0 copy-done.5
  14.9 0.6 fusion.50
  19.3 0.1 fusion.20
  19.4 0.0 copy-done.4
  19.4 0.4 select_reduce_fusion
  19.8 45.8 %all-to-all-done = bf16[8,21,9216]{2,1,0:T(8,128)(2,1)} async-done(((bf16[8,21,9216]{2,1,0:T(8,128)(2,1)}), bf16[8,21,9216]{2,1,0:T(8,128)(2,1)}, u32[]{:S(2)}, u32[]{:S(2)}) %all-to-all-start) | async-done | bytes 3096608 | tf_op jit(solution)/shard_map/all_to_all | solution.py:130
  65.7 1.5 slice_reduce_fusion
  67.2 0.1 reshape.861
  67.3 0.1 copy.20
  67.5 0.1 copy.21
  67.6 0.0 copy-start.3
  67.6 0.9 broadcast_in_dim.144
  68.6 3.5 %all-to-all-start.1 = ((bf16[8,96,512]{2,1,0:T(8,128)(2,1)}), bf16[8,96,512]{2,1,0:T(8,128)(2,1)S(1)}, u32[]{:S(2)}, u32[]{:S(2)}) async-start(bf16[8,96,512]{2,1,0:T(8,128)(2,1)} %broadcast_in_dim.144), calls=%async_computation.1 | async-start | bytes 1572864 | tf_op jit(solution)/shard_map/all_to_all | solution.py:135
  72.1 1.1 constant_dynamic-slice_fusion.1
  73.2 0.4 stack.30
  73.6 0.4 stack.31
  74.0 0.0 copy-done.3
  74.0 0.2 maximum_bitcast_fusion
  74.2 0.7 copy.22
  74.8 1.4 reshape.863.a_ref
  76.2 7.6 %all-to-all-done.1.p_ref = bf16[8,96,512]{2,1,0:T(8,128)(2,1)S(1)} async-done(((bf16[8,96,512]{2,1,0:T(8,128)(2,1)}), bf16[8,96,512]{2,1,0:T(8,128)(2,1)S(1)}, u32[]{:S(2)}, u32[]{:S(2)}) %all-to-all-start.1) | async-done | bytes 786464 | tf_op jit(solution)/shard_map/all_to_all | solution.py:135
  83.8 0.9 copy-done.2
  84.7 3.7 %partial.1 = (bf16[16,16,2304]{2,1,0:T(8,128)(2,1)}, f32[4,96,384]{2,1,0:T(8,128)}) custom-call(bf16[8,96,512]{2,1,0:T(8,128)(2,1)} %copy-done.2, bf16[96,512]{1,0:T(8,128)(2,1)} %copy-done.3, bf16[8,96,384]{2,1,0:T(8,128)(2,1)} %reshape.863.a_ref), custom_call_target="tpu_custom_call" | custom-call | tf_op jit(solution)/shard_map/partial/pallas_call | solution.py:145
  88.4 7.4 %all-to-all-start.2 = ((bf16[16,16,2304]{2,1,0:T(8,128)(2,1)}), bf16[16,16,2304]{2,1,0:T(8,128)(2,1)S(1)}, u32[]{:S(2)}, u32[]{:S(2)}) async-start(bf16[16,16,2304]{2,1,0:T(8,128)(2,1)} %get-tuple-element.7), calls=%async_computation.2 | async-start | bytes 2359296 | tf_op jit(solution)/shard_map/all_to_all | solution.py:156
  95.9 0.1 select_select_fusion
  95.9 0.1 reshape.858
  96.0 0.1 select_n.344
  96.1 0.1 fusion.24
  96.2 0.1 concatenate.21
  96.3 0.1 eq.166
  96.4 0.1 pad.23.clone
  96.4 0.1 add_add_fusion
  96.5 0.1 eq.154
  96.6 0.1 iota_add_fusion
  96.7 0.1 add.607
  96.8 18.4 %all-to-all-done.2 = bf16[16,16,2304]{2,1,0:T(8,128)(2,1)S(1)} async-done(((bf16[16,16,2304]{2,1,0:T(8,128)(2,1)}), bf16[16,16,2304]{2,1,0:T(8,128)(2,1)S(1)}, u32[]{:S(2)}, u32[]{:S(2)}) %all-to-all-start.2) | async-done | bytes 1179680 | tf_op jit(solution)/shard_map/all_to_all | solution.py:156
  115.2 0.5 fusion
  115.7 22.4 %all_to_all.25.r_ref = bf16[16,16,2304]{2,1,0:T(8,128)(2,1)} all-to-all(bf16[16,16,2304]{2,1,0:T(8,128)(2,1)S(1)} %bitcast.22), channel_id=1, replica_groups=mesh['row'=16,'col'=8] {'row'}, dimensions={0} | all-to-all | bytes 2359296 | tf_op jit(solution)/shard_map/all_to_all | solution.py:182
  138.1 3.8 %product.1 = bf16[384,1728]{1,0:T(8,128)(2,1)} custom-call(bf16[16,16,2304]{2,1,0:T(8,128)(2,1)} %all_to_all.25.r_ref, f32[4,96,384]{2,1,0:T(8,128)} %get-tuple-element.8.own_ref), custom_call_target="tpu_custom_call" | custom-call | tf_op jit(solution)/shard_map/product/pallas_call | solution.py:184
  142.0 3.6 %all-to-all-start.4 = ((bf16[8,48,1728]{2,1,0:T(8,128)(2,1)}), bf16[8,48,1728]{2,1,0:T(8,128)(2,1)S(1)}, u32[]{:S(2)}, u32[]{:S(2)}) async-start(bf16[8,48,1728]{2,1,0:T(8,128)(2,1)} %bitcast.20), calls=%async_computation.4 | async-start | bytes 2752512 | tf_op jit(solution)/shard_map/all_to_all | solution.py:192
  145.6 0.1 broadcast_add_fusion
  145.7 0.1 and_select_fusion.2
  145.8 0.4 select_reduce_fusion.1
  146.2 0.1 copy.16
  146.3 0.7 pad_add_fusion.1.j_ref
  147.0 20.4 %all-to-all-done.4.r_ref = bf16[8,48,1728]{2,1,0:T(8,128)(2,1)S(1)} async-done(((bf16[8,48,1728]{2,1,0:T(8,128)(2,1)}), bf16[8,48,1728]{2,1,0:T(8,128)(2,1)S(1)}, u32[]{:S(2)}, u32[]{:S(2)}) %all-to-all-start.4) | async-done | bytes 1327136 | tf_op jit(solution)/shard_map/all_to_all | solution.py:192
  167.4 1.1 copy-done.1
  168.5 4.1 %place.1 = f32[48,6144]{1,0:T(8,128)} custom-call(s32[8,18]{1,0:T(8,128)} %pad_add_fusion.1.j_ref, bf16[8,48,1728]{2,1,0:T(8,128)(2,1)} %copy-done.1), custom_call_target="tpu_custom_call" | custom-call | tf_op jit(solution)/shard_map/place/pallas_call | solution.py:201
  (27 shorter events, 0.3 us)
Async XLA Ops:
  0.0 6.0 %copy-start = (bf16[8,8,9216]{2,1,0:T(8,128)(2,1)S(1)}, bf16[8,8,9216]{2,1,0:T(8,128)(2,1)}, u32[]{:S(2)}) copy-start(bf16[8,8,9216]{2,1,0:T(8,128)(2,1)} %param.8) | copy-start | bytes 3538948
  8.8 6.1 %copy-start.5 = (s32[2]{0:T(128)S(1)}, s32[2]{0:T(128)}, u32[]{:S(2)}) copy-start(s32[2]{0:T(128)} %param.10) | copy-start | bytes 28
  8.8 10.6 %copy-start.4 = (s32[64]{0:T(128)S(1)}, s32[64]{0:T(128)}, u32[]{:S(2)}) copy-start(s32[64]{0:T(128)} %param.11) | copy-start | bytes 772
  8.8 56.9 %all-to-all-start = ((bf16[8,21,9216]{2,1,0:T(8,128)(2,1)}), bf16[8,21,9216]{2,1,0:T(8,128)(2,1)}, u32[]{:S(2)}, u32[]{:S(2)}) async-start(bf16[8,21,9216]{2,1,0:T(8,128)(2,1)} %pad_maximum_fusion), calls=%async_computation | async-start | bytes 7077888 | tf_op jit(solution)/shard_map/all_to_all | solution.py:130
  67.6 6.4 %copy-start.3 = (bf16[96,512]{1,0:T(8,128)(2,1)}, bf16[96,512]{1,0:T(8,128)(2,1)S(1)}, u32[]{:S(2)}) copy-start(bf16[96,512]{1,0:T(8,128)(2,1)S(1)} %pad.5.mine_ref) | copy-start | bytes 294916
  68.6 15.2 %all-to-all-start.1 = ((bf16[8,96,512]{2,1,0:T(8,128)(2,1)}), bf16[8,96,512]{2,1,0:T(8,128)(2,1)S(1)}, u32[]{:S(2)}, u32[]{:S(2)}) async-start(bf16[8,96,512]{2,1,0:T(8,128)(2,1)} %broadcast_in_dim.144), calls=%async_computation.1 | async-start | bytes 1572864 | tf_op jit(solution)/shard_map/all_to_all | solution.py:135
  83.8 0.9 copy-start.2
  88.4 26.8 %all-to-all-start.2 = ((bf16[16,16,2304]{2,1,0:T(8,128)(2,1)}), bf16[16,16,2304]{2,1,0:T(8,128)(2,1)S(1)}, u32[]{:S(2)}, u32[]{:S(2)}) async-start(bf16[16,16,2304]{2,1,0:T(8,128)(2,1)} %get-tuple-element.7), calls=%async_computation.2 | async-start | bytes 2359296 | tf_op jit(solution)/shard_map/all_to_all | solution.py:156
  142.0 25.4 %all-to-all-start.4 = ((bf16[8,48,1728]{2,1,0:T(8,128)(2,1)}), bf16[8,48,1728]{2,1,0:T(8,128)(2,1)S(1)}, u32[]{:S(2)}, u32[]{:S(2)}) async-start(bf16[8,48,1728]{2,1,0:T(8,128)(2,1)} %bitcast.20), calls=%async_computation.4 | async-start | bytes 2752512 | tf_op jit(solution)/shard_map/all_to_all | solution.py:192
  167.4 1.1 copy-start.1
